TPU v7x, 32 devices: a whole 2x2x4 slice. The times are simulated.
32 devices in a mesh: cell: 8 (over y, x, core), view: 4 (over z).
Axes of the slice: x: 2, y: 2, z: 4, core: 2. Of those that a mesh axis runs over, the one named last changes fastest.
Arguments:
- attributes: float32 [14, 65536], P(None, ('cell', 'view'))
- tile_anchor: float32 [2, 1536], P(None, ('cell', 'view')), may hold values from -2 to 4
- target: float32 [1536, 4, 256], P(('cell', 'view'))
- preconditioner: float32 [14, 14, 65536], P(None, None, ('cell', 'view')), as said below
- send_index: int32 [32, 32, 96], P(('cell', 'view')), may hold values from 0 to 2047, as said below
- tile_list: int32 [1536, 64], P(('cell', 'view')), may hold values from 0 to 3071, as said below
- pair_index: int32 [1536], P(('cell', 'view')), may hold values from 0 to 47, as said below
Outputs:
- update: float32 [14, 65536], P(None, ('cell', 'view'))
- step_residual: float32 [14, 65536], P(None, ('cell', 'view'))
Inputs may be any that keep to these rules, and one draw needn't show every extreme that they name: `send_index`: for each pair of devices, the 96 local Gaussian numbers that one sends to the other are distinct. `tile_list`: entries number a device's received rows by source device, then slot (96 a source); on each device the entries of its tiles are a permutation of those row numbers. `pair_index`: on each device, a permutation of its tiles' local numbers. `preconditioner`: each 14 x 14 block is symmetric and diagonally dominant with a positive diagonal.
All inputs are finite; a program needn't handle non-finite values.
Results may differ from a plain program's by a relative error of at most 0.0003.
Values sent between devices are 32-bit elements; how exact they have to be, the bound alone decides.
No kernel may reach another device: no remote copies, remote signals or barrier semaphores. Data moves between devices by JAX's collectives and lax.ppermute only.
A program may use at most 128 MiB of HBM per device.

v0:
```python
import math
import jax
import jax.numpy as jnp
from jax import lax
from jax.sharding import PartitionSpec as P

ITERS = 2
DAMPING = 0.5
PRIOR_WEIGHT = 0.3
DILATION = 0.3


def shifted(value, axis, by):
    devices = lax.axis_size(axis)
    return lax.ppermute(value, axis, [(i, (i + by) % devices) for i in range(devices)])


def camera_axes():
    tilt_cos, tilt_sin = (math.cos(0.3), math.sin(0.3))
    turn_cos, turn_sin = (math.cos(0.2), math.sin(0.2))
    return (
        (turn_cos, turn_sin * tilt_sin, turn_sin * tilt_cos),
        (0.0, tilt_cos, -tilt_sin),
        (-turn_sin, turn_cos * tilt_sin, turn_cos * tilt_cos),
    )


def render(listed, anchor):
    camera = camera_axes()
    factor_rows = (
        (jnp.exp(listed[3]), None, None),
        (listed[4], jnp.exp(listed[5]), None),
        (listed[6], listed[7], jnp.exp(listed[8])),
    )
    screen = []
    for axis_row in range(2):
        place_value = (
            camera[axis_row][0] * listed[0]
            + camera[axis_row][1] * listed[1]
            + camera[axis_row][2] * listed[2]
        )
        screen.append(place_value - anchor[axis_row][:, None])
    depth_values = camera[2][0] * listed[0] + camera[2][1] * listed[1] + camera[2][2] * listed[2]
    projected = []
    for axis_row in range(2):
        row_terms = []
        for column_index in range(3):
            total_term = camera[axis_row][column_index] * factor_rows[column_index][column_index]
            for inner_index in range(column_index + 1, 3):
                total_term = (
                    total_term
                    + camera[axis_row][inner_index] * factor_rows[inner_index][column_index]
                )
            row_terms.append(total_term)
        projected.append(row_terms)
    cov_xx = (
        projected[0][0] * projected[0][0]
        + projected[0][1] * projected[0][1]
        + projected[0][2] * projected[0][2]
        + DILATION
    )
    cov_xy = (
        projected[0][0] * projected[1][0]
        + projected[0][1] * projected[1][1]
        + projected[0][2] * projected[1][2]
    )
    cov_yy = (
        projected[1][0] * projected[1][0]
        + projected[1][1] * projected[1][1]
        + projected[1][2] * projected[1][2]
        + DILATION
    )
    determinant = cov_xx * cov_yy - cov_xy * cov_xy
    conic_xx = (cov_yy / determinant)[..., None]
    conic_xy = (-cov_xy / determinant)[..., None]
    conic_yy = (cov_xx / determinant)[..., None]
    opacity = 0.99 * jax.nn.sigmoid(listed[9])
    pixels = jnp.arange(256)
    pixel_x = (pixels % 16).astype(jnp.float32) + 0.5
    pixel_y = (pixels // 16).astype(jnp.float32) + 0.5
    offset_x = pixel_x - screen[0][:, :, None]
    offset_y = pixel_y - screen[1][:, :, None]
    exponent = -0.5 * (
        conic_xx * offset_x * offset_x
        + 2.0 * conic_xy * offset_x * offset_y
        + conic_yy * offset_y * offset_y
    )
    coverage = opacity[..., None] * jnp.exp(exponent)
    log_keep = jnp.log1p(-coverage)
    earlier = (jnp.arange(64)[None, :] < jnp.arange(64)[:, None]).astype(jnp.float32)
    before = jnp.einsum("jk,bkp->bjp", earlier, log_keep, precision=lax.Precision.HIGHEST)
    weight = jnp.exp(before) * coverage
    colours = jnp.einsum("cbk,bkp->bcp", listed[10:14], weight, precision=lax.Precision.HIGHEST)
    depths = jnp.einsum("bk,bkp->bp", depth_values, weight, precision=lax.Precision.HIGHEST)
    return (colours, depths)


def local(attributes, tile_anchor, target, preconditioner, send_index, tile_list, pair_index):
    cell_count = lax.axis_size("cell")
    view_count = lax.axis_size("view")
    devices = cell_count * view_count
    send_ids = send_index[0]
    slot_count = send_ids.shape[1]
    tiles_here = tile_list.shape[0]
    entries = tile_list.reshape(-1)
    entry_inverse = jnp.argsort(entries)
    pair_inverse = jnp.argsort(pair_index)

    def route(outgoing, forward):
        if forward:
            return lax.all_to_all(
                outgoing, ("cell", "view"), split_axis=1, concat_axis=1, tiled=True
            )
        return lax.all_to_all(outgoing, ("cell", "view"), split_axis=1, concat_axis=1, tiled=True)

    def deliver(values):
        received = route(values[:, send_ids], True)
        return received.reshape(14, -1)[:, entries].reshape(14, tiles_here, 64)

    def collect(cotangent):
        flattened = cotangent.reshape(14, -1)[:, entry_inverse].reshape(14, devices, slot_count)
        returned = route(flattened, False)
        summed = jax.ops.segment_sum(
            returned.reshape(14, -1).T, send_ids.reshape(-1), num_segments=attributes.shape[1]
        )
        return summed.T

    def neighbour(depth_map):
        return shifted(depth_map, "view", -1)[pair_index]

    def depth_cotangent(prior_term):
        arrived = shifted(prior_term[pair_inverse], "view", 1)
        return PRIOR_WEIGHT * prior_term - PRIOR_WEIGHT * arrived

    def apply_scaling(vector):
        return jnp.einsum("ijg,jg->ig", preconditioner, vector, precision=lax.Precision.HIGHEST)

    def global_inner(first, second):
        return lax.psum(jnp.sum(first * second), ("cell", "view"))

    def local_render(values):
        return render(values, tile_anchor)

    listed_now = deliver(attributes)
    (colours, depths), pull_fn = jax.vjp(local_render, listed_now)
    _, tangent_fn = jax.vjp(pull_fn, (jnp.zeros_like(colours), jnp.zeros_like(depths)))
    photometric = colours - target
    prior_term = PRIOR_WEIGHT * (depths - neighbour(depths))
    gradient = collect(pull_fn((photometric, depth_cotangent(prior_term)))[0])
    residual = -gradient
    solution = jnp.zeros_like(attributes)
    scaled = apply_scaling(residual)
    direction = scaled
    scaled_norm = global_inner(residual, scaled)
    for iteration in range(ITERS):
        colour_tangent, depth_tangent = tangent_fn((deliver(direction),))[0]
        prior_tangent = PRIOR_WEIGHT * (depth_tangent - neighbour(depth_tangent))
        normal_image = (
            collect(pull_fn((colour_tangent, depth_cotangent(prior_tangent)))[0])
            + DAMPING * direction
        )
        curvature_sum = lax.psum(jnp.sum(direction * normal_image), ("cell", "view"))
        step_size = scaled_norm / curvature_sum
        solution = solution + step_size * direction
        residual = residual - step_size * normal_image
        if iteration + 1 < ITERS:
            scaled = apply_scaling(residual)
            next_norm = global_inner(residual, scaled)
            direction = scaled + next_norm / scaled_norm * direction
            scaled_norm = next_norm
    return (solution, residual)


def solution(mesh):
    in_specs = (
        P(None, ("cell", "view")),
        P(None, ("cell", "view")),
        P(("cell", "view"), None, None),
        P(None, None, ("cell", "view")),
        P(("cell", "view"), None, None),
        P(("cell", "view"), None),
        P(("cell", "view")),
    )
    out_specs = (P(None, ("cell", "view")), P(None, ("cell", "view")))
    return jax.shard_map(local, mesh=mesh, in_specs=in_specs, out_specs=out_specs, check_vma=False)
```

profile of v0, /device:TPU:0, one launch (start us, length us, event | category | flops | bytes accessed | tf_op | source)
XLA Modules:
  0.0 688.7 jit_solution(14497731297453291714)
XLA Ops:
  2.7 8.1 %gather_fusion = f32[3072,14]{1,0:T(8,128)S(1)} fusion(f32[14,2048]{0,1:T(8,128)S(1)} %copy.404, s32[3072]{0:T(1024)S(1)} %broadcast_clamp_fusion.1), kind=kCustom, calls=%fused_computation | custom fusion | bytes 356352 | tf_op jit(solution)/shard_map/gather | solution.py:117
  12.1 7.3 %all-to-all-start = ((f32[14,32,96]{2,0,1:T(8,128)}), f32[14,32,96]{2,0,1:T(8,128)S(1)}, u32[]{:S(2)}, u32[]{:S(2)}) async-start(f32[14,32,96]{2,0,1:T(8,128)} %bitcast.2), calls=%async_computation | async-start | bytes 524288 | tf_op jit(solution)/shard_map/all_to_all | solution.py:111
  22.8 5.8 sort.35
  30.3 8.1 %gather_fusion.1 = f32[3072,14]{1,0:T(8,128)S(1)} fusion(f32[14,3072]{0,1:T(8,128)S(1)} %bitcast.428, s32[3072]{0:T(1024)S(1)} %broadcast_clamp_fusion), kind=kCustom, calls=%fused_computation.1 | custom fusion | bytes 356352 | tf_op jit(solution)/shard_map/gather | solution.py:118
  45.7 10.2 %bitcast_multiply_fusion.8 = (f32[48,64,256]{2,1,0:T(8,128)S(1)}, f32[48,256,64]{1,2,0:T(8,128)}) fusion(f32[48,64]{1,0:T(8,128)S(1)} %get-tuple-element.224, f32[48,64]{1,0:T(8,128)S(1)} %broadcast_subtract_fusion, f32[256]{0:T(256)S(1)} %copy-done.163, f32[48,64]{1,0:T(8,128)S(1)} %get-tuple-element.223, f32[48,64]{1,0:T(8,128)S(1)} %broadcast_subtract_fusion.1, ...), kind=kOutput, calls=%fused_computation.206 | convolution fusion | flops 624431104 | bytes 6367232 | tf_op jit(solution)/shard_map/jvp(jk,bkp->bjp)/dot_general | solution.py:91
  57.6 3.7 collective-permute-start
  62.9 3.4 fusion.336
  70.2 4.3 fusion.234
  86.9 2.7 fusion.226
  89.8 13.4 %fusion.44 = (f32[48,64]{1,0:T(8,128)S(1)}, f32[48,64]{1,0:T(8,128)S(1)}, f32[48,64]{1,0:T(8,128)S(1)}, f32[48,64]{1,0:T(8,128)S(1)}, f32[48,64]{1,0:T(8,128)S(1)}, /*index=5*/f32[48,64]{1,0:T(8,128)S(1)}) fusion(f32[48,64]{1,0:T(8,128)S(1)} %copy-done.81, f32[48,64]{1,0:T(8,128)S(1)} %copy-done.142, f32[256]{0:T(256)S(1)} %copy-done.164, ...), kind=kOutput, calls=%fused_computation.113 | convolution fusion | flops 651937792 | bytes 6502400 | tf_op jit(solution)/shard_map/transpose(jvp(jk,bkp->bjp))/dot_general | solution.py:91
  104.3 2.7 copy.465
  107.0 13.2 %gather_fusion.4 = f32[3072,14]{1,0:T(8,128)} fusion(f32[14,3072]{0,1:T(8,128)} %bitcast.431, s32[3072]{0:T(1024)} %fusion.294), kind=kCustom, calls=%fused_computation.4 | custom fusion | bytes 356352 | tf_op jit(solution)/shard_map/gather | solution.py:121
  120.3 2.6 copy.413
  122.9 6.2 all-to-all-start.1
  129.8 12.3 %copy.448 = f32[14,14,2048]{0,1,2:T(8,128)} copy(f32[14,14,2048]{2,1,0:T(8,128)} %param.10) | data formatting | bytes 3211264 | tf_op args[3]
  144.0 2.6 copy.415
  146.5 18.4 %scatter_custom_fusion = f32[2048,14]{1,0:T(8,128)} fusion(s32[3072]{0:T(1024)} %reshape.2786, f32[3072,14]{1,0:T(8,128)} %copy.415, f32[]{:T(128)} %constant.25.clone.1), kind=kCustom, calls=%fused_computation.298 | custom fusion | flops 43008 | bytes 115200 | tf_op jit(solution)/shard_map/scatter-add | solution.py:123
  166.2 17.7 %fusion.338 = f32[2048,1,14]{2,1,0:T(1,128)} fusion(f32[14,2048,1]{0,2,1:T(1,128)S(1)} %bitcast.433, f32[14,14,2048]{0,1,2:T(8,128)} %copy.448), kind=kOutput, calls=%fused_computation.628 | convolution fusion | flops 4816896 | bytes 1835008 | tf_op jit(solution)/shard_map/ijg,jg->ig/dot_general | solution.py:136
  183.9 12.0 %gather_fusion.5 = f32[3072,14]{1,0:T(8,128)} fusion(f32[14,2048]{0,1:T(8,128)} %bitcast.419, s32[3072]{0:T(1024)S(1)} %broadcast_clamp_fusion.1), kind=kCustom, calls=%fused_computation.5 | custom fusion | bytes 356352 | tf_op jit(solution)/shard_map/gather | solution.py:117
  196.0 2.6 copy.416
  198.6 16.1 %all_to_all.30 = f32[14,32,96]{2,0,1:T(8,128)} all-to-all(f32[14,32,96]{2,0,1:T(8,128)} %bitcast.447), channel_id=1, replica_groups=mesh['cell'=8,'view'=4] {'cell','view'}, dimensions={1} | all-to-all | bytes 344064 | tf_op jit(solution)/shard_map/all_to_all | solution.py:111
  214.7 2.6 copy.417
  217.3 12.2 %gather_fusion.6 = f32[3072,14]{1,0:T(8,128)} fusion(f32[14,3072]{0,1:T(8,128)} %bitcast.429, s32[3072]{0:T(1024)S(1)} %copy-done.90), kind=kCustom, calls=%fused_computation.6 | custom fusion | bytes 356352 | tf_op jit(solution)/shard_map/gather | solution.py:118
  229.6 2.6 copy.418
  232.2 3.2 add_reduce_fusion.5
  256.2 14.3 %fusion.53 = f32[48,64,256]{2,1,0:T(8,128)S(1)} fusion(f32[48,256,64]{1,2,0:T(8,128)S(1)} %copy-done.174, f32[48,64]{1,0:T(8,128)S(1)} %copy-done.158, f32[48,64]{1,0:T(8,128)S(1)} %get-tuple-element.189, f32[48,64]{1,0:T(8,128)S(1)} %neg.806, f32[48,64]{1,0:T(8,128)S(1)} %copy-done.160, f32[48,64]{1,0:T(8,128)S(1)} %get-tuple-element.188, ...), kind=kOutput, calls=%fused_computation.122 | convolution fusion | flops 663752704 | bytes 6477824 | tf_op jit(solution)/shard_map/transpose(jvp(transpose(jvp(jk,bkp->bjp))))/dot_general | solution.py:91
  270.6 2.4 fusion.341
  280.1 3.3 fusion.339
  287.4 2.7 fusion.231
  290.2 3.0 collective-permute-done.3
  293.3 13.3 %fusion.55 = (f32[48,64]{1,0:T(8,128)S(1)}, f32[48,64]{1,0:T(8,128)S(1)}, f32[48,64]{1,0:T(8,128)S(1)}, f32[48,64]{1,0:T(8,128)S(1)}, f32[48,64]{1,0:T(8,128)S(1)}, /*index=5*/f32[48,64]{1,0:T(8,128)S(1)}) fusion(f32[48,64]{1,0:T(8,128)S(1)} %copy-done.83, f32[48,64]{1,0:T(8,128)S(1)} %copy-done.144, f32[256]{0:T(256)S(1)} %copy-done.166, ...), kind=kOutput, calls=%fused_computation.124 | convolution fusion | flops 651937792 | bytes 6502400 | tf_op jit(solution)/shard_map/transpose(jvp(jk,bkp->bjp))/dot_general | solution.py:91
  306.8 2.7 fusion.224
  310.5 2.7 copy.467
  313.2 13.2 %gather_fusion.9 = f32[3072,14]{1,0:T(8,128)} fusion(f32[14,3072]{0,1:T(8,128)} %bitcast.432, s32[3072]{0:T(1024)} %fusion.294), kind=kCustom, calls=%fused_computation.9 | custom fusion | bytes 356352 | tf_op jit(solution)/shard_map/gather | solution.py:121
  326.4 2.6 copy.425
  329.0 12.8 %all_to_all.31 = f32[14,32,96]{2,0,1:T(8,128)S(1)} all-to-all(f32[14,32,96]{2,0,1:T(8,128)} %copy.425), channel_id=1, replica_groups=mesh['cell'=8,'view'=4] {'cell','view'}, dimensions={1} | all-to-all | bytes 344064 | tf_op jit(solution)/shard_map/all_to_all | solution.py:114
  342.8 2.6 copy.427
  345.3 18.3 %scatter_custom_fusion.1 = f32[2048,14]{1,0:T(8,128)} fusion(s32[3072]{0:T(1024)} %reshape.2786, f32[3072,14]{1,0:T(8,128)} %copy.427, f32[]{:T(128)} %constant.25.clone.1), kind=kCustom, calls=%fused_computation.296 | custom fusion | flops 43008 | bytes 115200 | tf_op jit(solution)/shard_map/scatter-add | solution.py:123
  363.6 2.8 multiply_reduce_fusion.5
  366.4 38.6 %all-reduce.51 = (f32[]{:T(128)}, f32[]{:T(128)}) all-reduce(f32[]{:T(128)} %get-tuple-element.35, f32[]{:T(128)} %get-tuple-element.34), channel_id=1, replica_groups=mesh['cell'=8,'view'=4] {'cell','view'}, use_global_device_ids=true, to_apply=%region_10.11 | all-reduce | flops 2 | bytes 16 | tf_op jit(solution)/shard_map/psum | solution.py:139
  408.3 17.4 %fusion.342 = f32[2048,1,14]{2,1,0:T(1,128)S(1)} fusion(f32[14,2048,1]{0,2,1:T(1,128)S(1)} %bitcast.424, f32[14,14,2048]{0,1,2:T(8,128)} %copy.448), kind=kOutput, calls=%fused_computation.632 | convolution fusion | flops 4816896 | bytes 1835008 | tf_op jit(solution)/shard_map/ijg,jg->ig/dot_general | solution.py:136
  427.7 40.6 %psum.30 = f32[]{:T(128)} all-reduce(f32[]{:T(128)} %multiply_reduce_fusion.4), channel_id=1, replica_groups=mesh['cell'=8,'view'=4] {'cell','view'}, use_global_device_ids=true, to_apply=%region_21.22 | all-reduce | flops 1 | bytes 8 | tf_op jit(solution)/shard_map/psum | solution.py:139
  469.6 2.6 multiply_add_fusion.7
  472.2 12.1 %gather_fusion.10 = f32[3072,14]{1,0:T(8,128)} fusion(f32[14,2048]{0,1:T(8,128)} %multiply_add_fusion.7, s32[3072]{0:T(1024)S(1)} %broadcast_clamp_fusion.1), kind=kCustom, calls=%fused_computation.10 | custom fusion | bytes 356352 | tf_op jit(solution)/shard_map/gather | solution.py:117
  484.2 2.6 copy.428
  486.9 14.7 %all_to_all.32 = f32[14,32,96]{2,0,1:T(8,128)} all-to-all(f32[14,32,96]{2,0,1:T(8,128)} %bitcast.448), channel_id=1, replica_groups=mesh['cell'=8,'view'=4] {'cell','view'}, dimensions={1} | all-to-all | bytes 344064 | tf_op jit(solution)/shard_map/all_to_all | solution.py:111
  501.6 2.6 copy.429
  504.2 12.4 %gather_fusion.11 = f32[3072,14]{1,0:T(8,128)} fusion(f32[14,3072]{0,1:T(8,128)} %bitcast.427, s32[3072]{0:T(1024)S(1)} %copy-done.91), kind=kCustom, calls=%fused_computation.11 | custom fusion | bytes 356352 | tf_op jit(solution)/shard_map/gather | solution.py:118
  516.6 2.6 copy.430
  519.2 3.3 add_reduce_fusion.4
  544.1 13.7 %fusion.64 = f32[48,64,256]{2,1,0:T(8,128)S(1)} fusion(f32[48,256,64]{1,2,0:T(8,128)S(1)} %copy-done.176, f32[48,64]{1,0:T(8,128)S(1)} %copy-done.157, f32[48,64]{1,0:T(8,128)S(1)} %get-tuple-element.185, f32[48,64]{1,0:T(8,128)S(1)} %copy-done.108, f32[48,64]{1,0:T(8,128)S(1)} %get-tuple-element.202, f32[48,64]{1,0:T(8,128)S(1)} %get-tuple-element.184, ...), kind=kOutput, calls=%fused_computation.133 | convolution fusion | flops 663752704 | bytes 6477824 | tf_op jit(solution)/shard_map/transpose(jvp(transpose(jvp(jk,bkp->bjp))))/dot_general | solution.py:91
  557.8 2.4 fusion.345
  562.5 2.3 fusion.344
  566.8 3.3 fusion.343
  574.0 2.7 fusion.228
  576.8 3.0 collective-permute-done.5
  579.9 13.3 %fusion.66 = (f32[48,64]{1,0:T(8,128)S(1)}, f32[48,64]{1,0:T(8,128)S(1)}, f32[48,64]{1,0:T(8,128)S(1)}, f32[48,64]{1,0:T(8,128)S(1)}, f32[48,64]{1,0:T(8,128)S(1)}, /*index=5*/f32[48,64]{1,0:T(8,128)S(1)}) fusion(f32[48,64]{1,0:T(8,128)S(1)} %copy-done.86, f32[48,64]{1,0:T(8,128)S(1)} %copy-done.146, f32[256]{0:T(256)S(1)} %copy-done.168, ...), kind=kOutput, calls=%fused_computation.135 | convolution fusion | flops 651937792 | bytes 6502400 | tf_op jit(solution)/shard_map/transpose(jvp(jk,bkp->bjp))/dot_general | solution.py:91
  593.3 2.7 fusion.222
  596.9 8.1 %gather_fusion.14 = f32[3072,14]{1,0:T(8,128)S(1)} fusion(f32[14,3072]{0,1:T(8,128)S(1)} %bitcast.430, s32[3072]{0:T(1024)S(1)} %copy-done.88), kind=kCustom, calls=%fused_computation.14 | custom fusion | bytes 356352 | tf_op jit(solution)/shard_map/gather | solution.py:121
  605.5 12.1 %all_to_all.33 = f32[14,32,96]{2,0,1:T(8,128)S(1)} all-to-all(f32[14,32,96]{2,0,1:T(8,128)S(1)} %copy.437), channel_id=1, replica_groups=mesh['cell'=8,'view'=4] {'cell','view'}, dimensions={1} | all-to-all | bytes 344064 | tf_op jit(solution)/shard_map/all_to_all | solution.py:114
  618.5 2.6 copy.439
  621.1 18.3 %scatter_custom_fusion.2 = f32[2048,14]{1,0:T(8,128)} fusion(s32[3072]{0:T(1024)} %reshape.2786, f32[3072,14]{1,0:T(8,128)} %copy.439, f32[]{:T(128)} %constant.25.clone.1), kind=kCustom, calls=%fused_computation.294 | custom fusion | flops 43008 | bytes 115200 | tf_op jit(solution)/shard_map/scatter-add | solution.py:123
  641.5 38.5 %psum.31 = f32[]{:T(128)} all-reduce(f32[]{:T(128)} %multiply_reduce_fusion.3), channel_id=1, replica_groups=mesh['cell'=8,'view'=4] {'cell','view'}, use_global_device_ids=true, to_apply=%region_30.31 | all-reduce | flops 1 | bytes 8 | tf_op jit(solution)/shard_map/psum | solution.py:162
  681.3 2.8 multiply_subtract_fusion
  (534 shorter events, 115.2 us)
Async XLA Ops:
  0.6 19.3 %copy-start.104 = (s32[48,64]{1,0:T(8,128)S(1)}, s32[48,64]{1,0:T(8,128)}, u32[]{:S(2)}) copy-start(s32[48,64]{1,0:T(8,128)} %param.12) | copy-start | bytes 36868
  0.6 19.5 %copy-start.161 = (f32[2,48]{1,0:T(2,128)S(1)}, f32[2,48]{1,0:T(2,128)}, u32[]{:S(2)}) copy-start(f32[2,48]{1,0:T(2,128)} %param.8) | copy-start | bytes 1156
  0.7 19.5 %copy-start.162 = (s32[48]{0:T(128)S(1)}, s32[48]{0:T(128)}, u32[]{:S(2)}) copy-start(s32[48]{0:T(128)} %param.13) | copy-start | bytes 580
  12.1 17.7 %all-to-all-start = ((f32[14,32,96]{2,0,1:T(8,128)}), f32[14,32,96]{2,0,1:T(8,128)S(1)}, u32[]{:S(2)}, u32[]{:S(2)}) async-start(f32[14,32,96]{2,0,1:T(8,128)} %bitcast.2), calls=%async_computation | async-start | bytes 524288 | tf_op jit(solution)/shard_map/all_to_all | solution.py:111
  20.1 23.4 %copy-start.89 = (s32[3072]{0:T(1024)}, s32[3072]{0:T(1024)S(1)}, u32[]{:S(2)}) copy-start(s32[3072]{0:T(1024)S(1)} %broadcast_clamp_fusion) | copy-start | bytes 36868
  29.8 15.9 %copy-start.163 = (f32[256]{0:T(256)S(1)}, f32[256]{0:T(256)}, u32[]{:S(2)}) copy-start(f32[256]{0:T(256)} %fusion.299) | copy-start | bytes 3076
  43.8 12.1 %copy-start.135 = (f32[48,64]{1,0:T(8,128)}, f32[48,64]{1,0:T(8,128)S(1)}, u32[]{:S(2)}) copy-start(f32[48,64]{1,0:T(8,128)S(1)} %broadcast_multiply_fusion.3) | copy-start | bytes 36868
  57.6 8.7 %collective-permute-start = (f32[48,256]{1,0:T(8,128)S(1)}, f32[48,256]{1,0:T(8,128)S(1)}, u32[]{:S(2)}, u32[]{:S(2)}) collective-permute-start(f32[48,256]{1,0:T(8,128)S(1)} %bitcast.471), channel_id=1, source_target_pairs={{0,3},{1,0},{2,1},{3,2},{4,7},{5,4},{6,5},{7,6},{8,11},{9,8},{10,9... | collective-permute-start | bytes 147464 | tf_op jit(solution)/shard_map/ppermute | solution.py:15
  69.7 16.3 %collective-permute-start.1 = (f32[48,256]{1,0:T(8,128)}, f32[48,256]{1,0:T(8,128)}, u32[]{:S(2)}, u32[]{:S(2)}) collective-permute-start(f32[48,256]{1,0:T(8,128)} %gather_fusion.3), channel_id=1, source_target_pairs={{0,1},{1,2},{2,3},{3,0},{4,5},{5,6},{6,7},{7,4},{8,9},{9,10},{10,1... | collective-permute-start | bytes 147464 | tf_op jit(solution)/shard_map/ppermute | solution.py:15
  74.5 15.1 %copy-start.69 = (f32[48,64]{1,0:T(8,128)S(1)}, f32[48,64]{1,0:T(8,128)}, u32[]{:S(2)}) copy-start(f32[48,64]{1,0:T(8,128)} %copy-done.68) | copy-start | bytes 36868
  74.5 15.1 %copy-start.75 = (f32[48,64]{1,0:T(8,128)S(1)}, f32[48,64]{1,0:T(8,128)}, u32[]{:S(2)}) copy-start(f32[48,64]{1,0:T(8,128)} %copy-done.74) | copy-start | bytes 36868
  74.5 15.1 %copy-start.81 = (f32[48,64]{1,0:T(8,128)S(1)}, f32[48,64]{1,0:T(8,128)}, u32[]{:S(2)}) copy-start(f32[48,64]{1,0:T(8,128)} %copy-done.80) | copy-start | bytes 36868
  75.9 27.6 %copy-start.56 = (f32[1,48,64]{2,1,0:T(8,128)}, f32[1,48,64]{2,1,0:T(8,128)S(1)}, u32[]{:S(2)}) copy-start(f32[1,48,64]{2,1,0:T(8,128)S(1)} %div.471) | copy-start | bytes 36868
  76.0 27.3 %copy-start.16 = (f32[1,48,64]{2,1,0:T(8,128)}, f32[1,48,64]{2,1,0:T(8,128)S(1)}, u32[]{:S(2)}) copy-start(f32[1,48,64]{2,1,0:T(8,128)S(1)} %exp.339) | copy-start | bytes 36868
  76.8 26.7 %copy-start.19 = (f32[1,48,64]{2,1,0:T(8,128)}, f32[1,48,64]{2,1,0:T(8,128)S(1)}, u32[]{:S(2)}) copy-start(f32[1,48,64]{2,1,0:T(8,128)S(1)} %exp.340) | copy-start | bytes 36868
  77.6 25.8 %copy-start.22 = (f32[1,48,64]{2,1,0:T(8,128)}, f32[1,48,64]{2,1,0:T(8,128)S(1)}, u32[]{:S(2)}) copy-start(f32[1,48,64]{2,1,0:T(8,128)S(1)} %exp.341) | copy-start | bytes 36868
  89.7 13.4 %copy-start.98 = (f32[1,48,64]{2,1,0:T(8,128)S(1)}, f32[1,48,64]{2,1,0:T(8,128)}, u32[]{:S(2)}) copy-start(f32[1,48,64]{2,1,0:T(8,128)} %mul.5873) | copy-start | bytes 36868
  89.7 13.4 %copy-start.99 = (f32[1,48,64]{2,1,0:T(8,128)S(1)}, f32[1,48,64]{2,1,0:T(8,128)}, u32[]{:S(2)}) copy-start(f32[1,48,64]{2,1,0:T(8,128)} %mul.5874) | copy-start | bytes 36868
  89.7 13.4 %copy-start.100 = (f32[1,48,64]{2,1,0:T(8,128)S(1)}, f32[1,48,64]{2,1,0:T(8,128)}, u32[]{:S(2)}) copy-start(f32[1,48,64]{2,1,0:T(8,128)} %mul.5877) | copy-start | bytes 36868
  89.8 13.4 %copy-start.101 = (f32[1,48,64]{2,1,0:T(8,128)S(1)}, f32[1,48,64]{2,1,0:T(8,128)}, u32[]{:S(2)}) copy-start(f32[1,48,64]{2,1,0:T(8,128)} %mul.5882) | copy-start | bytes 36868
  89.8 13.4 %copy-start.102 = (f32[1,48,64]{2,1,0:T(8,128)S(1)}, f32[1,48,64]{2,1,0:T(8,128)}, u32[]{:S(2)}) copy-start(f32[1,48,64]{2,1,0:T(8,128)} %mul.5883) | copy-start | bytes 36868
  89.8 13.4 %copy-start.103 = (f32[1,48,64]{2,1,0:T(8,128)S(1)}, f32[1,48,64]{2,1,0:T(8,128)}, u32[]{:S(2)}) copy-start(f32[1,48,64]{2,1,0:T(8,128)} %mul.5886) | copy-start | bytes 36868
  89.8 13.8 %copy-start.52 = (f32[48,4,64]{2,0,1:T(8,128)S(1)}, f32[48,4,64]{2,0,1:T(8,128)}, u32[]{:S(2)}) copy-start(f32[48,4,64]{2,0,1:T(8,128)} %copy.510) | copy-start | bytes 147460
  103.3 19.6 %copy-start.34 = (f32[1,48,64]{2,1,0:T(8,128)}, f32[1,48,64]{2,1,0:T(8,128)S(1)}, u32[]{:S(2)}) copy-start(f32[1,48,64]{2,1,0:T(8,128)S(1)} %get-tuple-element.129) | copy-start | bytes 36868
  103.3 19.6 %copy-start.37 = (f32[1,48,64]{2,1,0:T(8,128)}, f32[1,48,64]{2,1,0:T(8,128)S(1)}, u32[]{:S(2)}) copy-start(f32[1,48,64]{2,1,0:T(8,128)S(1)} %get-tuple-element.132) | copy-start | bytes 36868
  103.3 19.6 %copy-start.40 = (f32[1,48,64]{2,1,0:T(8,128)}, f32[1,48,64]{2,1,0:T(8,128)S(1)}, u32[]{:S(2)}) copy-start(f32[1,48,64]{2,1,0:T(8,128)S(1)} %get-tuple-element.125) | copy-start | bytes 36868
  103.3 19.6 %copy-start.43 = (f32[1,48,64]{2,1,0:T(8,128)}, f32[1,48,64]{2,1,0:T(8,128)S(1)}, u32[]{:S(2)}) copy-start(f32[1,48,64]{2,1,0:T(8,128)S(1)} %get-tuple-element.126) | copy-start | bytes 36868
  103.3 19.6 %copy-start.46 = (f32[1,48,64]{2,1,0:T(8,128)}, f32[1,48,64]{2,1,0:T(8,128)S(1)}, u32[]{:S(2)}) copy-start(f32[1,48,64]{2,1,0:T(8,128)S(1)} %get-tuple-element.127) | copy-start | bytes 36868
  103.3 19.6 %copy-start.49 = (f32[1,48,64]{2,1,0:T(8,128)}, f32[1,48,64]{2,1,0:T(8,128)S(1)}, u32[]{:S(2)}) copy-start(f32[1,48,64]{2,1,0:T(8,128)S(1)} %get-tuple-element.128) | copy-start | bytes 36868
  104.3 24.8 %copy-start.131 = (s32[1,32,96]{2,1,0:T(8,128)S(1)}, s32[1,32,96]{2,1,0:T(8,128)}, u32[]{:S(2)}) copy-start(s32[1,32,96]{2,1,0:T(8,128)} %param.11) | copy-start | bytes 36868
  122.9 19.2 %all-to-all-start.1 = ((f32[14,32,96]{2,0,1:T(8,128)}), f32[14,32,96]{2,0,1:T(8,128)}, u32[]{:S(2)}, u32[]{:S(2)}) async-start(f32[14,32,96]{2,0,1:T(8,128)} %copy.413), calls=%async_computation.1 | async-start | bytes 524288 | tf_op jit(solution)/shard_map/all_to_all | solution.py:114
  183.9 33.4 %copy-start.90 = (s32[3072]{0:T(1024)S(1)}, s32[3072]{0:T(1024)}, u32[]{:S(2)}) copy-start(s32[3072]{0:T(1024)} %copy-done.89) | copy-start | bytes 36868
  198.6 39.7 %copy-start.54 = (f32[48,64]{1,0:T(8,128)S(1)}, f32[48,64]{1,0:T(8,128)}, u32[]{:S(2)}) copy-start(f32[48,64]{1,0:T(8,128)} %copy-done.53) | copy-start | bytes 36868
  198.6 41.8 %copy-start.70 = (f32[48,64]{1,0:T(8,128)S(1)}, f32[48,64]{1,0:T(8,128)}, u32[]{:S(2)}) copy-start(f32[48,64]{1,0:T(8,128)} %copy-done.68) | copy-start | bytes 36868
  198.6 41.8 %copy-start.76 = (f32[48,64]{1,0:T(8,128)S(1)}, f32[48,64]{1,0:T(8,128)}, u32[]{:S(2)}) copy-start(f32[48,64]{1,0:T(8,128)} %copy-done.74) | copy-start | bytes 36868
  214.7 26.3 %copy-start.95 = (f32[1,3072]{1,0:T(1,128)S(1)}, f32[1,3072]{1,0:T(1,128)}, u32[]{:S(2)}) copy-start(f32[1,3072]{1,0:T(1,128)} %get-tuple-element.154) | copy-start | bytes 36868
  214.7 37.1 %copy-start.82 = (f32[48,64]{1,0:T(8,128)S(1)}, f32[48,64]{1,0:T(8,128)}, u32[]{:S(2)}) copy-start(f32[48,64]{1,0:T(8,128)} %copy-done.80) | copy-start | bytes 36868
  229.5 25.6 %copy-start.8 = (f32[48,64]{1,0:T(8,128)S(1)}, f32[48,64]{1,0:T(8,128)}, u32[]{:S(2)}) copy-start(f32[48,64]{1,0:T(8,128)} %copy-done.7) | copy-start | bytes 36868
  229.5 25.6 %copy-start.11 = (f32[48,64]{1,0:T(8,128)S(1)}, f32[48,64]{1,0:T(8,128)}, u32[]{:S(2)}) copy-start(f32[48,64]{1,0:T(8,128)} %copy-done.10) | copy-start | bytes 36868
  229.5 25.7 %copy-start.14 = (f32[48,64]{1,0:T(8,128)S(1)}, f32[48,64]{1,0:T(8,128)}, u32[]{:S(2)}) copy-start(f32[48,64]{1,0:T(8,128)} %copy-done.13) | copy-start | bytes 36868
  229.5 25.7 %copy-start.60 = (f32[48,64]{1,0:T(8,128)S(1)}, f32[48,64]{1,0:T(8,128)}, u32[]{:S(2)}) copy-start(f32[48,64]{1,0:T(8,128)} %copy-done.59) | copy-start | bytes 36868
  229.5 25.7 %copy-start.63 = (f32[48,64]{1,0:T(8,128)S(1)}, f32[48,64]{1,0:T(8,128)}, u32[]{:S(2)}) copy-start(f32[48,64]{1,0:T(8,128)} %copy-done.62) | copy-start | bytes 36868
  256.2 14.4 %copy-start.32 = (f32[48,64,1]{1,0,2:T(8,128)S(1)}, f32[48,64,1]{1,0,2:T(8,128)}, u32[]{:S(2)}) copy-start(f32[48,64,1]{1,0,2:T(8,128)} %copy-done.31) | copy-start | bytes 36868
  278.4 5.1 collective-permute-start.2
  287.0 6.2 collective-permute-start.3
  293.3 13.4 %copy-start.57 = (f32[1,48,64]{2,1,0:T(8,128)S(1)}, f32[1,48,64]{2,1,0:T(8,128)}, u32[]{:S(2)}) copy-start(f32[1,48,64]{2,1,0:T(8,128)} %copy-done.56) | copy-start | bytes 36868
  408.3 17.4 %copy-start.2 = (f32[14,2048]{0,1:T(8,128)}, f32[14,2048]{0,1:T(8,128)S(1)}, u32[]{:S(2)}) copy-start(f32[14,2048]{0,1:T(8,128)S(1)} %bitcast_subtract_fusion) | copy-start | bytes 344068
  472.2 32.0 %copy-start.91 = (s32[3072]{0:T(1024)S(1)}, s32[3072]{0:T(1024)}, u32[]{:S(2)}) copy-start(s32[3072]{0:T(1024)} %copy-done.89) | copy-start | bytes 36868
  486.9 39.3 %copy-start.96 = (f32[1,3072]{1,0:T(1,128)S(1)}, f32[1,3072]{1,0:T(1,128)}, u32[]{:S(2)}) copy-start(f32[1,3072]{1,0:T(1,128)} %get-tuple-element.154) | copy-start | bytes 36868
  486.9 39.3 %copy-start.97 = (f32[1,3072]{1,0:T(1,128)S(1)}, f32[1,3072]{1,0:T(1,128)}, u32[]{:S(2)}) copy-start(f32[1,3072]{1,0:T(1,128)} %get-tuple-element.156) | copy-start | bytes 36868
  501.6 38.7 %copy-start.84 = (f32[48,64]{1,0:T(8,128)S(1)}, f32[48,64]{1,0:T(8,128)}, u32[]{:S(2)}) copy-start(f32[48,64]{1,0:T(8,128)} %copy-done.80) | copy-start | bytes 36868
  516.6 27.1 %copy-start.55 = (f32[48,64]{1,0:T(8,128)S(1)}, f32[48,64]{1,0:T(8,128)}, u32[]{:S(2)}) copy-start(f32[48,64]{1,0:T(8,128)} %copy-done.53) | copy-start | bytes 36868
  516.6 27.1 %copy-start.9 = (f32[48,64]{1,0:T(8,128)S(1)}, f32[48,64]{1,0:T(8,128)}, u32[]{:S(2)}) copy-start(f32[48,64]{1,0:T(8,128)} %copy-done.7) | copy-start | bytes 36868
  516.6 27.1 %copy-start.12 = (f32[48,64]{1,0:T(8,128)S(1)}, f32[48,64]{1,0:T(8,128)}, u32[]{:S(2)}) copy-start(f32[48,64]{1,0:T(8,128)} %copy-done.10) | copy-start | bytes 36868
  516.6 27.1 %copy-start.15 = (f32[48,64]{1,0:T(8,128)S(1)}, f32[48,64]{1,0:T(8,128)}, u32[]{:S(2)}) copy-start(f32[48,64]{1,0:T(8,128)} %copy-done.13) | copy-start | bytes 36868
  516.6 27.1 %copy-start.61 = (f32[48,64]{1,0:T(8,128)S(1)}, f32[48,64]{1,0:T(8,128)}, u32[]{:S(2)}) copy-start(f32[48,64]{1,0:T(8,128)} %copy-done.59) | copy-start | bytes 36868
  516.6 27.1 %copy-start.64 = (f32[48,64]{1,0:T(8,128)S(1)}, f32[48,64]{1,0:T(8,128)}, u32[]{:S(2)}) copy-start(f32[48,64]{1,0:T(8,128)} %copy-done.62) | copy-start | bytes 36868
  544.1 13.7 %copy-start.33 = (f32[48,64,1]{1,0,2:T(8,128)S(1)}, f32[48,64,1]{1,0,2:T(8,128)}, u32[]{:S(2)}) copy-start(f32[48,64,1]{1,0,2:T(8,128)} %copy-done.31) | copy-start | bytes 36868
  564.8 5.3 collective-permute-start.4
  573.6 6.2 collective-permute-start.5
  579.9 13.4 %copy-start.58 = (f32[1,48,64]{2,1,0:T(8,128)S(1)}, f32[1,48,64]{2,1,0:T(8,128)}, u32[]{:S(2)}) copy-start(f32[1,48,64]{2,1,0:T(8,128)} %copy-done.56) | copy-start | bytes 36868
  605.0 34.3 %copy-start.1 = (f32[14,2048]{0,1:T(8,128)S(1)}, f32[14,2048]{0,1:T(8,128)}, u32[]{:S(2)}) copy-start(f32[14,2048]{0,1:T(8,128)} %multiply_add_fusion.7) | copy-start | bytes 344068
  605.5 75.7 %copy-start = (f32[2048,1,14]{2,1,0:T(1,128)S(1)}, f32[2048,1,14]{2,1,0:T(1,128)}, u32[]{:S(2)}) copy-start(f32[2048,1,14]{2,1,0:T(1,128)} %fusion.338) | copy-start | bytes 344068
  605.5 75.7 %copy-start.3 = (f32[14,2048]{0,1:T(8,128)S(1)}, f32[14,2048]{0,1:T(8,128)}, u32[]{:S(2)}) copy-start(f32[14,2048]{0,1:T(8,128)} %copy-done.2) | copy-start | bytes 344068
  (122 other events, 476.2 us)
where the time goes:
time: 701 us; the launch traced here: 689 us
  local copies, waits for them, and re-layouts  215 us (31%)
  blocking collectives  173 us (25%)
  matrix products  160 us (23%)
  other arithmetic  105 us (15%)
  starting transfers between devices  22.1 us (3%)
  between operations  7.35 us (1%)
    psum x2, blocking collectives, global_inner(): return lax.psum(jnp.sum(first * second), ('cell', 'view'))  79.2 us
    dot_general x6, matrix products, render(): jnp.einsum('jk,bkp->bjp', earlier, log_keep, precision=lax.Precision.HIGH...  78.2 us
    all_to_all x4, blocking collectives, route(): lax.all_to_all(outgoing, ('cell', 'view'), split_axis=1, concat_axis=1, t...  55.7 us
    scatter-add x3, other arithmetic, collect(): jax.ops.segment_sum(returned.reshape(14, -1).T, send_ids.reshape(-1), num...  54.9 us
    gather x6, local copies, waits for them, and re-layouts, deliver(): received = route(values[:, send_ids], True)  38.6 us
    psum x1, blocking collectives, local(): lax.psum(jnp.sum(direction * normal_image), ('cell', 'view'))  38.5 us
    gather x6, local copies, waits for them, and re-layouts, deliver(): return received.reshape(14, -1)[:, entries].reshape(14, tiles_here, 64)  38.4 us
    dot_general x2, matrix products, apply_scaling(): jnp.einsum('ijg,jg->ig', preconditioner, vector, precision=lax.Precision....  35.2 us
  transfers between devices with their start and end apart: 8, of which 2 were waited for; matrix products, arithmetic and copies ran while one was open for 8% of the time, Pallas kernels for 0%

commit v1 on v0

--- a/solution.py
+++ b/solution.py
@@ -108,8 +108,14 @@
 
     def route(outgoing, forward):
         if forward:
-            return lax.all_to_all(
-                outgoing, ("cell", "view"), split_axis=1, concat_axis=1, tiled=True
+            return jnp.concatenate(
+                lax.all_to_all(
+                    jnp.stack(jnp.split(outgoing, lax.axis_size(("cell", "view")), axis=1)),
+                    ("cell", "view"),
+                    0,
+                    0,
+                ),
+                axis=1,
             )
         return lax.all_to_all(outgoing, ("cell", "view"), split_axis=1, concat_axis=1, tiled=True)
 

time: 701 us -> 729 us (1.040)
  local copies, waits for them, and re-layouts: 215 us -> 233 us
  starting transfers between devices: 22.1 us -> 33.5 us
    all_to_all x4 -> x2, blocking collectives: 55.7 us -> 24.9 us  [route(): lax.all_to_all(outgoing, ('cell', 'view'), split_axis=1, concat_axis=1, t...]
    all_to_all x0 -> x2, blocking collectives: none -> 29.3 us  [route(): lax.all_to_all(jnp.stack(jnp.split(outgoing, lax.axis_size(('cell', 'view...]
    unnamed x360 -> x459, local copies, waits for them, and re-layouts: 21.2 us -> 41.6 us
    ppermute x6, starting transfers between devices: 8.63 us -> 20 us  [shifted(): lax.ppermute(value, axis, [(i, (i + by) % devices) for i in range(devices)])]
    all_to_all x2 -> x1, starting transfers between devices: 13.5 us -> 6.16 us  [route(): lax.all_to_all(outgoing, ('cell', 'view'), split_axis=1, concat_axis=1, t...]
    all_to_all x0 -> x1, starting transfers between devices: none -> 7.33 us  [route(): lax.all_to_all(jnp.stack(jnp.split(outgoing, lax.axis_size(('cell', 'view...]
where the time goes in v1:
time: 729 us; the launch traced here: 717 us
  local copies, waits for them, and re-layouts  233 us (32%)
  blocking collectives  172 us (24%)
  matrix products  159 us (22%)
  other arithmetic  105 us (14%)
  starting transfers between devices  33.5 us (5%)
  between operations  7.95 us (1%)
    psum x2, blocking collectives, global_inner(): return lax.psum(jnp.sum(first * second), ('cell', 'view'))  79.3 us
    dot_general x6, matrix products, render(): jnp.einsum('jk,bkp->bjp', earlier, log_keep, precision=lax.Precision.HIGH...  76.8 us
    scatter-add x3, other arithmetic, collect(): jax.ops.segment_sum(returned.reshape(14, -1).T, send_ids.reshape(-1), num...  55.1 us
    unnamed x459, local copies, waits for them, and re-layouts  41.6 us
    gather x6, local copies, waits for them, and re-layouts, deliver(): return received.reshape(14, -1)[:, entries].reshape(14, tiles_here, 64)  39.8 us
    psum x1, blocking collectives, local(): lax.psum(jnp.sum(direction * normal_image), ('cell', 'view'))  38.5 us
    gather x6, local copies, waits for them, and re-layouts, deliver(): received = route(values[:, send_ids], True)  36.6 us
    dot_general x2, matrix products, apply_scaling(): jnp.einsum('ijg,jg->ig', preconditioner, vector, precision=lax.Precision....  35.2 us
  transfers between devices with their start and end apart: 8, of which 2 were waited for; matrix products, arithmetic and copies ran while one was open for 8% of the time, Pallas kernels for 0%

profile of v1, /device:TPU:0, one launch (start us, length us, event | category | flops | bytes accessed | tf_op | source)
XLA Modules:
  0.0 716.7 jit_solution(8774722237358631193)
XLA Ops:
  2.7 8.1 %gather_fusion = f32[3072,14]{1,0:T(8,128)S(1)} fusion(f32[14,2048]{0,1:T(8,128)S(1)} %copy.716, s32[3072]{0:T(1024)S(1)} %broadcast_clamp_fusion.1), kind=kCustom, calls=%fused_computation | custom fusion | bytes 356352 | tf_op jit(solution)/shard_map/gather | solution.py:123
  30.7 7.3 %all-to-all-start = ((f32[32,14,1,96]{3,2,1,0:T(1,128)}), f32[32,14,1,96]{3,2,1,0:T(1,128)S(1)}, u32[]{:S(2)}, u32[]{:S(2)}) async-start(f32[32,14,1,96]{3,2,1,0:T(1,128)} %constant_dynamic-update-slice_fusion), calls=%async_computation | async-start | bytes 458752 | tf_op jit(solution)/shard_map/all_to_all | solution.py:112
  41.5 5.8 sort.35
  49.1 8.1 %gather_fusion.1 = f32[3072,14]{1,0:T(8,128)S(1)} fusion(f32[14,3072]{0,1:T(8,128)S(1)} %bitcast.815, s32[3072]{0:T(1024)S(1)} %broadcast_clamp_fusion), kind=kCustom, calls=%fused_computation.1 | custom fusion | bytes 356352 | tf_op jit(solution)/shard_map/gather | solution.py:124
  58.2 2.2 fusion.330
  64.5 10.2 %bitcast_multiply_fusion.8 = (f32[48,64,256]{2,1,0:T(8,128)S(1)}, f32[48,256,64]{1,2,0:T(8,128)}) fusion(f32[48,64]{1,0:T(8,128)S(1)} %get-tuple-element.226, f32[48,64]{1,0:T(8,128)S(1)} %broadcast_subtract_fusion, f32[256]{0:T(256)S(1)} %copy-done.166, f32[48,64]{1,0:T(8,128)S(1)} %get-tuple-element.225, f32[48,64]{1,0:T(8,128)S(1)} %broadcast_subtract_fusion.1, ...), kind=kOutput, calls=%fused_computation.206 | convolution fusion | flops 624431104 | bytes 6367232 | tf_op jit(solution)/shard_map/jvp(jk,bkp->bjp)/dot_general | solution.py:91
  76.4 3.7 collective-permute-start
  81.7 3.4 fusion.336
  88.4 11.6 %collective-permute-start.1 = (f32[48,256]{1,0:T(8,128)}, f32[48,256]{1,0:T(8,128)}, u32[]{:S(2)}, u32[]{:S(2)}) collective-permute-start(f32[48,256]{1,0:T(8,128)} %gather_fusion.3), channel_id=1, source_target_pairs={{0,1},{1,2},{2,3},{3,0},{4,5},{5,6},{6,7},{7,4},{8,9},{9,10},{10,1... | collective-permute-start | bytes 147464 | tf_op jit(solution)/shard_map/ppermute | solution.py:15
  100.0 4.3 fusion.234
  116.8 2.7 fusion.226
  119.6 13.4 %fusion.44 = (f32[48,64]{1,0:T(8,128)S(1)}, f32[48,64]{1,0:T(8,128)S(1)}, f32[48,64]{1,0:T(8,128)S(1)}, f32[48,64]{1,0:T(8,128)S(1)}, f32[48,64]{1,0:T(8,128)S(1)}, /*index=5*/f32[48,64]{1,0:T(8,128)S(1)}) fusion(f32[48,64]{1,0:T(8,128)S(1)} %copy-done.81, f32[48,64]{1,0:T(8,128)S(1)} %copy-done.145, f32[256]{0:T(256)S(1)} %copy-done.167, ...), kind=kOutput, calls=%fused_computation.113 | convolution fusion | flops 651937792 | bytes 6502400 | tf_op jit(solution)/shard_map/transpose(jvp(jk,bkp->bjp))/dot_general | solution.py:91
  134.2 2.7 copy.777
  136.9 13.2 %gather_fusion.4 = f32[3072,14]{1,0:T(8,128)} fusion(f32[14,3072]{0,1:T(8,128)} %bitcast.818, s32[3072]{0:T(1024)} %fusion.294), kind=kCustom, calls=%fused_computation.4 | custom fusion | bytes 356352 | tf_op jit(solution)/shard_map/gather | solution.py:127
  150.1 2.6 copy.725
  152.8 6.2 all-to-all-start.1
  159.6 12.3 %copy.760 = f32[14,14,2048]{0,1,2:T(8,128)} copy(f32[14,14,2048]{2,1,0:T(8,128)} %param.10) | data formatting | bytes 3211264 | tf_op args[3]
  173.8 2.6 copy.727
  176.4 18.2 %scatter_custom_fusion = f32[2048,14]{1,0:T(8,128)} fusion(s32[3072]{0:T(1024)} %reshape.2786, f32[3072,14]{1,0:T(8,128)} %copy.727, f32[]{:T(128)} %constant.25.clone.1), kind=kCustom, calls=%fused_computation.298 | custom fusion | flops 43008 | bytes 115200 | tf_op jit(solution)/shard_map/scatter-add | solution.py:129
  195.9 17.7 %fusion.338 = f32[2048,1,14]{2,1,0:T(1,128)} fusion(f32[14,2048,1]{0,2,1:T(1,128)S(1)} %bitcast.820, f32[14,14,2048]{0,1,2:T(8,128)} %copy.760), kind=kOutput, calls=%fused_computation.820 | convolution fusion | flops 4816896 | bytes 1835008 | tf_op jit(solution)/shard_map/ijg,jg->ig/dot_general | solution.py:142
  213.6 12.0 %gather_fusion.5 = f32[3072,14]{1,0:T(8,128)} fusion(f32[14,2048]{0,1:T(8,128)} %bitcast.806, s32[3072]{0:T(1024)S(1)} %broadcast_clamp_fusion.1), kind=kCustom, calls=%fused_computation.5 | custom fusion | bytes 356352 | tf_op jit(solution)/shard_map/gather | solution.py:123
  228.2 15.3 %all_to_all.30 = f32[32,14,1,96]{3,2,1,0:T(1,128)S(1)} all-to-all(f32[32,14,1,96]{3,2,1,0:T(1,128)S(1)} %constant_dynamic-update-slice_fusion.32), channel_id=1, replica_groups=mesh['cell'=8,'view'=4] {'cell','view'}, dimensions={0} | all-to-all | bytes 344064 | tf_op jit(solution)/shard_map/all_to_all | solution.py:112
  245.2 13.6 %gather_fusion.6 = f32[3072,14]{1,0:T(8,128)} fusion(f32[14,3072]{0,1:T(8,128)} %bitcast.816, s32[3072]{0:T(1024)} %copy-done.91), kind=kCustom, calls=%fused_computation.6 | custom fusion | bytes 356352 | tf_op jit(solution)/shard_map/gather | solution.py:124
  258.9 2.6 copy.730
  261.4 3.1 add_reduce_fusion.5
  288.1 13.5 %fusion.53 = f32[48,64,256]{2,1,0:T(8,128)S(1)} fusion(f32[48,256,64]{1,2,0:T(8,128)S(1)} %copy-done.177, f32[48,64]{1,0:T(8,128)S(1)} %copy-done.161, f32[48,64]{1,0:T(8,128)S(1)} %get-tuple-element.191, f32[48,64]{1,0:T(8,128)S(1)} %copy-done.110, f32[48,64]{1,0:T(8,128)S(1)} %copy-done.163, f32[48,64]{1,0:T(8,128)S(1)} %get-tuple-element.190, ...), kind=kOutput, calls=%fused_computation.122 | convolution fusion | flops 663752704 | bytes 6477824 | tf_op jit(solution)/shard_map/transpose(jvp(transpose(jvp(jk,bkp->bjp))))/dot_general | solution.py:91
  301.6 2.4 fusion.341
  307.0 2.3 fusion.340
  311.2 3.3 fusion.339
  318.6 2.7 fusion.231
  321.4 2.9 collective-permute-done.3
  324.4 13.2 %fusion.55 = (f32[48,64]{1,0:T(8,128)S(1)}, f32[48,64]{1,0:T(8,128)S(1)}, f32[48,64]{1,0:T(8,128)S(1)}, f32[48,64]{1,0:T(8,128)S(1)}, f32[48,64]{1,0:T(8,128)S(1)}, /*index=5*/f32[48,64]{1,0:T(8,128)S(1)}) fusion(f32[48,64]{1,0:T(8,128)S(1)} %copy-done.84, f32[48,64]{1,0:T(8,128)S(1)} %copy-done.147, f32[256]{0:T(256)S(1)} %copy-done.169, ...), kind=kOutput, calls=%fused_computation.124 | convolution fusion | flops 651937792 | bytes 6502400 | tf_op jit(solution)/shard_map/transpose(jvp(jk,bkp->bjp))/dot_general | solution.py:91
  337.7 2.7 fusion.224
  341.4 2.7 copy.779
  344.1 13.2 %gather_fusion.9 = f32[3072,14]{1,0:T(8,128)} fusion(f32[14,3072]{0,1:T(8,128)} %bitcast.819, s32[3072]{0:T(1024)} %fusion.294), kind=kCustom, calls=%fused_computation.9 | custom fusion | bytes 356352 | tf_op jit(solution)/shard_map/gather | solution.py:127
  357.3 2.6 copy.737
  360.0 12.8 %all_to_all.31 = f32[14,32,96]{2,0,1:T(8,128)S(1)} all-to-all(f32[14,32,96]{2,0,1:T(8,128)} %copy.737), channel_id=1, replica_groups=mesh['cell'=8,'view'=4] {'cell','view'}, dimensions={1} | all-to-all | bytes 344064 | tf_op jit(solution)/shard_map/all_to_all | solution.py:120
  373.7 2.6 copy.739
  376.2 18.6 %scatter_custom_fusion.1 = f32[2048,14]{1,0:T(8,128)} fusion(s32[3072]{0:T(1024)} %reshape.2786, f32[3072,14]{1,0:T(8,128)} %copy.739, f32[]{:T(128)} %constant.25.clone.1), kind=kCustom, calls=%fused_computation.296 | custom fusion | flops 43008 | bytes 115200 | tf_op jit(solution)/shard_map/scatter-add | solution.py:129
  394.9 2.8 multiply_reduce_fusion.5
  397.7 38.6 %all-reduce.51 = (f32[]{:T(128)}, f32[]{:T(128)}) all-reduce(f32[]{:T(128)} %get-tuple-element.37, f32[]{:T(128)} %get-tuple-element.36), channel_id=1, replica_groups=mesh['cell'=8,'view'=4] {'cell','view'}, use_global_device_ids=true, to_apply=%region_10.11 | all-reduce | flops 2 | bytes 16 | tf_op jit(solution)/shard_map/psum | solution.py:145
  439.7 17.4 %fusion.342 = f32[2048,1,14]{2,1,0:T(1,128)S(1)} fusion(f32[14,2048,1]{0,2,1:T(1,128)S(1)} %bitcast.811, f32[14,14,2048]{0,1,2:T(8,128)} %copy.760), kind=kOutput, calls=%fused_computation.824 | convolution fusion | flops 4816896 | bytes 1835008 | tf_op jit(solution)/shard_map/ijg,jg->ig/dot_general | solution.py:142
  459.0 40.6 %psum.30 = f32[]{:T(128)} all-reduce(f32[]{:T(128)} %multiply_reduce_fusion.4), channel_id=1, replica_groups=mesh['cell'=8,'view'=4] {'cell','view'}, use_global_device_ids=true, to_apply=%region_21.22 | all-reduce | flops 1 | bytes 8 | tf_op jit(solution)/shard_map/psum | solution.py:145
  500.9 2.6 multiply_add_fusion.7
  503.5 12.1 %gather_fusion.10 = f32[3072,14]{1,0:T(8,128)} fusion(f32[14,2048]{0,1:T(8,128)} %multiply_add_fusion.7, s32[3072]{0:T(1024)S(1)} %broadcast_clamp_fusion.1), kind=kCustom, calls=%fused_computation.10 | custom fusion | bytes 356352 | tf_op jit(solution)/shard_map/gather | solution.py:123
  518.2 13.9 %all_to_all.32 = f32[32,14,1,96]{3,2,1,0:T(1,128)S(1)} all-to-all(f32[32,14,1,96]{3,2,1,0:T(1,128)S(1)} %constant_dynamic-update-slice_fusion.64), channel_id=1, replica_groups=mesh['cell'=8,'view'=4] {'cell','view'}, dimensions={0} | all-to-all | bytes 344064 | tf_op jit(solution)/shard_map/all_to_all | solution.py:112
  533.7 12.4 %gather_fusion.11 = f32[3072,14]{1,0:T(8,128)} fusion(f32[14,3072]{0,1:T(8,128)} %bitcast.814, s32[3072]{0:T(1024)S(1)} %copy-done.92), kind=kCustom, calls=%fused_computation.11 | custom fusion | bytes 356352 | tf_op jit(solution)/shard_map/gather | solution.py:124
  546.1 2.6 copy.742
  548.7 3.3 add_reduce_fusion.4
  572.2 13.5 %fusion.64 = f32[48,64,256]{2,1,0:T(8,128)S(1)} fusion(f32[48,256,64]{1,2,0:T(8,128)S(1)} %copy-done.179, f32[48,64]{1,0:T(8,128)S(1)} %copy-done.160, f32[48,64]{1,0:T(8,128)S(1)} %get-tuple-element.187, f32[48,64]{1,0:T(8,128)S(1)} %copy-done.108, f32[48,64]{1,0:T(8,128)S(1)} %get-tuple-element.204, f32[48,64]{1,0:T(8,128)S(1)} %get-tuple-element.186, ...), kind=kOutput, calls=%fused_computation.133 | convolution fusion | flops 663752704 | bytes 6477824 | tf_op jit(solution)/shard_map/transpose(jvp(transpose(jvp(jk,bkp->bjp))))/dot_general | solution.py:91
  585.7 2.4 fusion.345
  590.4 2.3 fusion.344
  594.6 3.3 fusion.343
  602.0 2.7 fusion.228
  604.7 2.9 collective-permute-done.5
  607.8 13.2 %fusion.66 = (f32[48,64]{1,0:T(8,128)S(1)}, f32[48,64]{1,0:T(8,128)S(1)}, f32[48,64]{1,0:T(8,128)S(1)}, f32[48,64]{1,0:T(8,128)S(1)}, f32[48,64]{1,0:T(8,128)S(1)}, /*index=5*/f32[48,64]{1,0:T(8,128)S(1)}) fusion(f32[48,64]{1,0:T(8,128)S(1)} %copy-done.87, f32[48,64]{1,0:T(8,128)S(1)} %copy-done.149, f32[256]{0:T(256)S(1)} %copy-done.171, ...), kind=kOutput, calls=%fused_computation.135 | convolution fusion | flops 651937792 | bytes 6502400 | tf_op jit(solution)/shard_map/transpose(jvp(jk,bkp->bjp))/dot_general | solution.py:91
  621.1 2.7 fusion.222
  624.6 8.1 %gather_fusion.14 = f32[3072,14]{1,0:T(8,128)S(1)} fusion(f32[14,3072]{0,1:T(8,128)S(1)} %bitcast.817, s32[3072]{0:T(1024)S(1)} %copy-done.90), kind=kCustom, calls=%fused_computation.14 | custom fusion | bytes 356352 | tf_op jit(solution)/shard_map/gather | solution.py:127
  633.3 12.1 %all_to_all.33 = f32[14,32,96]{2,0,1:T(8,128)S(1)} all-to-all(f32[14,32,96]{2,0,1:T(8,128)S(1)} %copy.749), channel_id=1, replica_groups=mesh['cell'=8,'view'=4] {'cell','view'}, dimensions={1} | all-to-all | bytes 344064 | tf_op jit(solution)/shard_map/all_to_all | solution.py:120
  646.3 2.6 copy.751
  648.9 18.3 %scatter_custom_fusion.2 = f32[2048,14]{1,0:T(8,128)} fusion(s32[3072]{0:T(1024)} %reshape.2786, f32[3072,14]{1,0:T(8,128)} %copy.751, f32[]{:T(128)} %constant.25.clone.1), kind=kCustom, calls=%fused_computation.294 | custom fusion | flops 43008 | bytes 115200 | tf_op jit(solution)/shard_map/scatter-add | solution.py:129
  669.2 38.5 %psum.31 = f32[]{:T(128)} all-reduce(f32[]{:T(128)} %multiply_reduce_fusion.3), channel_id=1, replica_groups=mesh['cell'=8,'view'=4] {'cell','view'}, use_global_device_ids=true, to_apply=%region_30.31 | all-reduce | flops 1 | bytes 8 | tf_op jit(solution)/shard_map/psum | solution.py:168
  709.1 2.8 multiply_subtract_fusion
  711.9 2.2 copy.752
  (636 shorter events, 136.3 us)
Async XLA Ops:
  0.6 37.9 %copy-start.104 = (s32[48,64]{1,0:T(8,128)S(1)}, s32[48,64]{1,0:T(8,128)}, u32[]{:S(2)}) copy-start(s32[48,64]{1,0:T(8,128)} %param.12) | copy-start | bytes 36868
  0.6 38.1 %copy-start.164 = (f32[2,48]{1,0:T(2,128)S(1)}, f32[2,48]{1,0:T(2,128)}, u32[]{:S(2)}) copy-start(f32[2,48]{1,0:T(2,128)} %param.8) | copy-start | bytes 1156
  0.7 38.2 %copy-start.165 = (s32[48]{0:T(128)S(1)}, s32[48]{0:T(128)}, u32[]{:S(2)}) copy-start(s32[48]{0:T(128)} %param.13) | copy-start | bytes 580
  30.7 17.7 %all-to-all-start = ((f32[32,14,1,96]{3,2,1,0:T(1,128)}), f32[32,14,1,96]{3,2,1,0:T(1,128)S(1)}, u32[]{:S(2)}, u32[]{:S(2)}) async-start(f32[32,14,1,96]{3,2,1,0:T(1,128)} %constant_dynamic-update-slice_fusion), calls=%async_computation | async-start | bytes 458752 | tf_op jit(solution)/shard_map/all_to_all | solution.py:112
  38.8 23.6 %copy-start.91 = (s32[3072]{0:T(1024)}, s32[3072]{0:T(1024)S(1)}, u32[]{:S(2)}) copy-start(s32[3072]{0:T(1024)S(1)} %broadcast_clamp_fusion) | copy-start | bytes 36868
  48.4 16.1 %copy-start.166 = (f32[256]{0:T(256)S(1)}, f32[256]{0:T(256)}, u32[]{:S(2)}) copy-start(f32[256]{0:T(256)} %fusion.299) | copy-start | bytes 3076
  76.4 8.7 %collective-permute-start = (f32[48,256]{1,0:T(8,128)S(1)}, f32[48,256]{1,0:T(8,128)S(1)}, u32[]{:S(2)}, u32[]{:S(2)}) collective-permute-start(f32[48,256]{1,0:T(8,128)S(1)} %bitcast.955), channel_id=1, source_target_pairs={{0,3},{1,0},{2,1},{3,2},{4,7},{5,4},{6,5},{7,6},{8,11},{9,8},{10,9... | collective-permute-start | bytes 147464 | tf_op jit(solution)/shard_map/ppermute | solution.py:15
  88.4 15.9 %copy-start.65 = (f32[48,4,64]{2,1,0:T(4,128)S(1)}, f32[48,4,64]{2,1,0:T(4,128)}, u32[]{:S(2)}) copy-start(f32[48,4,64]{2,1,0:T(4,128)} %fusion.336) | copy-start | bytes 147460
  88.4 16.6 %copy-start.136 = (f32[3072]{0:T(1024)S(1)}, f32[3072]{0:T(1024)}, u32[]{:S(2)}) copy-start(f32[3072]{0:T(1024)} %get-tuple-element.135) | copy-start | bytes 36868
  88.4 17.3 %copy-start.137 = (f32[1,3072]{1,0:T(1,128)S(1)}, f32[1,3072]{1,0:T(1,128)}, u32[]{:S(2)}) copy-start(f32[1,3072]{1,0:T(1,128)} %get-tuple-element.138) | copy-start | bytes 36868
  88.4 17.3 %copy-start.135 = (f32[3072]{0:T(1024)S(1)}, f32[3072]{0:T(1024)}, u32[]{:S(2)}) copy-start(f32[3072]{0:T(1024)} %get-tuple-element.172) | copy-start | bytes 36868
  88.4 27.3 %collective-permute-start.1 = (f32[48,256]{1,0:T(8,128)}, f32[48,256]{1,0:T(8,128)}, u32[]{:S(2)}, u32[]{:S(2)}) collective-permute-start(f32[48,256]{1,0:T(8,128)} %gather_fusion.3), channel_id=1, source_target_pairs={{0,1},{1,2},{2,3},{3,0},{4,5},{5,6},{6,7},{7,4},{8,9},{9,10},{10,1... | collective-permute-start | bytes 147464 | tf_op jit(solution)/shard_map/ppermute | solution.py:15
  104.4 15.1 %copy-start.68 = (f32[48,64]{1,0:T(8,128)S(1)}, f32[48,64]{1,0:T(8,128)}, u32[]{:S(2)}) copy-start(f32[48,64]{1,0:T(8,128)} %copy-done.67) | copy-start | bytes 36868
  104.4 15.1 %copy-start.74 = (f32[48,64]{1,0:T(8,128)S(1)}, f32[48,64]{1,0:T(8,128)}, u32[]{:S(2)}) copy-start(f32[48,64]{1,0:T(8,128)} %copy-done.73) | copy-start | bytes 36868
  104.4 15.1 %copy-start.81 = (f32[48,64]{1,0:T(8,128)S(1)}, f32[48,64]{1,0:T(8,128)}, u32[]{:S(2)}) copy-start(f32[48,64]{1,0:T(8,128)} %copy-done.80) | copy-start | bytes 36868
  105.8 27.6 %copy-start.55 = (f32[1,48,64]{2,1,0:T(8,128)}, f32[1,48,64]{2,1,0:T(8,128)S(1)}, u32[]{:S(2)}) copy-start(f32[1,48,64]{2,1,0:T(8,128)S(1)} %div.471) | copy-start | bytes 36868
  105.9 27.3 %copy-start.16 = (f32[1,48,64]{2,1,0:T(8,128)}, f32[1,48,64]{2,1,0:T(8,128)S(1)}, u32[]{:S(2)}) copy-start(f32[1,48,64]{2,1,0:T(8,128)S(1)} %exp.339) | copy-start | bytes 36868
  106.7 26.7 %copy-start.19 = (f32[1,48,64]{2,1,0:T(8,128)}, f32[1,48,64]{2,1,0:T(8,128)S(1)}, u32[]{:S(2)}) copy-start(f32[1,48,64]{2,1,0:T(8,128)S(1)} %exp.340) | copy-start | bytes 36868
  107.4 25.8 %copy-start.22 = (f32[1,48,64]{2,1,0:T(8,128)}, f32[1,48,64]{2,1,0:T(8,128)S(1)}, u32[]{:S(2)}) copy-start(f32[1,48,64]{2,1,0:T(8,128)S(1)} %exp.341) | copy-start | bytes 36868
  119.6 13.4 %copy-start.98 = (f32[1,48,64]{2,1,0:T(8,128)S(1)}, f32[1,48,64]{2,1,0:T(8,128)}, u32[]{:S(2)}) copy-start(f32[1,48,64]{2,1,0:T(8,128)} %mul.5873) | copy-start | bytes 36868
  119.6 13.4 %copy-start.99 = (f32[1,48,64]{2,1,0:T(8,128)S(1)}, f32[1,48,64]{2,1,0:T(8,128)}, u32[]{:S(2)}) copy-start(f32[1,48,64]{2,1,0:T(8,128)} %mul.5874) | copy-start | bytes 36868
  119.6 13.4 %copy-start.100 = (f32[1,48,64]{2,1,0:T(8,128)S(1)}, f32[1,48,64]{2,1,0:T(8,128)}, u32[]{:S(2)}) copy-start(f32[1,48,64]{2,1,0:T(8,128)} %mul.5877) | copy-start | bytes 36868
  119.6 13.4 %copy-start.101 = (f32[1,48,64]{2,1,0:T(8,128)S(1)}, f32[1,48,64]{2,1,0:T(8,128)}, u32[]{:S(2)}) copy-start(f32[1,48,64]{2,1,0:T(8,128)} %mul.5882) | copy-start | bytes 36868
  119.6 13.4 %copy-start.102 = (f32[1,48,64]{2,1,0:T(8,128)S(1)}, f32[1,48,64]{2,1,0:T(8,128)}, u32[]{:S(2)}) copy-start(f32[1,48,64]{2,1,0:T(8,128)} %mul.5883) | copy-start | bytes 36868
  119.6 13.8 %copy-start.52 = (f32[48,4,64]{2,0,1:T(8,128)S(1)}, f32[48,4,64]{2,0,1:T(8,128)}, u32[]{:S(2)}) copy-start(f32[48,4,64]{2,0,1:T(8,128)} %copy.822) | copy-start | bytes 147460
  133.1 19.6 %copy-start.34 = (f32[1,48,64]{2,1,0:T(8,128)}, f32[1,48,64]{2,1,0:T(8,128)S(1)}, u32[]{:S(2)}) copy-start(f32[1,48,64]{2,1,0:T(8,128)S(1)} %get-tuple-element.131) | copy-start | bytes 36868
  133.1 19.6 %copy-start.37 = (f32[1,48,64]{2,1,0:T(8,128)}, f32[1,48,64]{2,1,0:T(8,128)S(1)}, u32[]{:S(2)}) copy-start(f32[1,48,64]{2,1,0:T(8,128)S(1)} %get-tuple-element.134) | copy-start | bytes 36868
  133.1 19.6 %copy-start.40 = (f32[1,48,64]{2,1,0:T(8,128)}, f32[1,48,64]{2,1,0:T(8,128)S(1)}, u32[]{:S(2)}) copy-start(f32[1,48,64]{2,1,0:T(8,128)S(1)} %get-tuple-element.127) | copy-start | bytes 36868
  133.2 19.6 %copy-start.43 = (f32[1,48,64]{2,1,0:T(8,128)}, f32[1,48,64]{2,1,0:T(8,128)S(1)}, u32[]{:S(2)}) copy-start(f32[1,48,64]{2,1,0:T(8,128)S(1)} %get-tuple-element.128) | copy-start | bytes 36868
  133.2 19.6 %copy-start.46 = (f32[1,48,64]{2,1,0:T(8,128)}, f32[1,48,64]{2,1,0:T(8,128)S(1)}, u32[]{:S(2)}) copy-start(f32[1,48,64]{2,1,0:T(8,128)S(1)} %get-tuple-element.129) | copy-start | bytes 36868
  133.2 19.6 %copy-start.49 = (f32[1,48,64]{2,1,0:T(8,128)}, f32[1,48,64]{2,1,0:T(8,128)S(1)}, u32[]{:S(2)}) copy-start(f32[1,48,64]{2,1,0:T(8,128)S(1)} %get-tuple-element.130) | copy-start | bytes 36868
  134.2 24.8 %copy-start.133 = (s32[1,32,96]{2,1,0:T(8,128)S(1)}, s32[1,32,96]{2,1,0:T(8,128)}, u32[]{:S(2)}) copy-start(s32[1,32,96]{2,1,0:T(8,128)} %param.11) | copy-start | bytes 36868
  152.8 19.2 %all-to-all-start.1 = ((f32[14,32,96]{2,0,1:T(8,128)}), f32[14,32,96]{2,0,1:T(8,128)}, u32[]{:S(2)}, u32[]{:S(2)}) async-start(f32[14,32,96]{2,0,1:T(8,128)} %copy.725), calls=%async_computation.1 | async-start | bytes 524288 | tf_op jit(solution)/shard_map/all_to_all | solution.py:120
  245.2 23.8 %copy-start.69 = (f32[48,64]{1,0:T(8,128)S(1)}, f32[48,64]{1,0:T(8,128)}, u32[]{:S(2)}) copy-start(f32[48,64]{1,0:T(8,128)} %copy-done.67) | copy-start | bytes 36868
  245.2 23.8 %copy-start.75 = (f32[48,64]{1,0:T(8,128)S(1)}, f32[48,64]{1,0:T(8,128)}, u32[]{:S(2)}) copy-start(f32[48,64]{1,0:T(8,128)} %copy-done.73) | copy-start | bytes 36868
  245.2 39.2 %copy-start.82 = (f32[48,64]{1,0:T(8,128)S(1)}, f32[48,64]{1,0:T(8,128)}, u32[]{:S(2)}) copy-start(f32[48,64]{1,0:T(8,128)} %copy-done.80) | copy-start | bytes 36868
  258.8 28.9 %copy-start.8 = (f32[48,64]{1,0:T(8,128)S(1)}, f32[48,64]{1,0:T(8,128)}, u32[]{:S(2)}) copy-start(f32[48,64]{1,0:T(8,128)} %copy-done.7) | copy-start | bytes 36868
  258.8 28.9 %copy-start.11 = (f32[48,64]{1,0:T(8,128)S(1)}, f32[48,64]{1,0:T(8,128)}, u32[]{:S(2)}) copy-start(f32[48,64]{1,0:T(8,128)} %copy-done.10) | copy-start | bytes 36868
  258.8 28.9 %copy-start.14 = (f32[48,64]{1,0:T(8,128)S(1)}, f32[48,64]{1,0:T(8,128)}, u32[]{:S(2)}) copy-start(f32[48,64]{1,0:T(8,128)} %copy-done.13) | copy-start | bytes 36868
  258.8 28.9 %copy-start.59 = (f32[48,64]{1,0:T(8,128)S(1)}, f32[48,64]{1,0:T(8,128)}, u32[]{:S(2)}) copy-start(f32[48,64]{1,0:T(8,128)} %copy-done.58) | copy-start | bytes 36868
  258.8 28.9 %copy-start.62 = (f32[48,64]{1,0:T(8,128)S(1)}, f32[48,64]{1,0:T(8,128)}, u32[]{:S(2)}) copy-start(f32[48,64]{1,0:T(8,128)} %copy-done.61) | copy-start | bytes 36868
  269.0 14.7 %copy-start.111 = (f32[48,64]{1,0:T(8,128)}, f32[48,64]{1,0:T(8,128)S(1)}, u32[]{:S(2)}) copy-start(f32[48,64]{1,0:T(8,128)S(1)} %neg.803) | copy-start | bytes 36868
  288.1 13.5 %copy-start.32 = (f32[48,64,1]{1,0,2:T(8,128)S(1)}, f32[48,64,1]{1,0,2:T(8,128)}, u32[]{:S(2)}) copy-start(f32[48,64,1]{1,0,2:T(8,128)} %copy-done.31) | copy-start | bytes 36868
  309.4 5.2 collective-permute-start.2
  318.1 6.2 collective-permute-start.3
  439.7 17.5 %copy-start.2 = (f32[14,2048]{0,1:T(8,128)}, f32[14,2048]{0,1:T(8,128)S(1)}, u32[]{:S(2)}) copy-start(f32[14,2048]{0,1:T(8,128)S(1)} %bitcast_subtract_fusion) | copy-start | bytes 344068
  503.5 30.2 %copy-start.92 = (s32[3072]{0:T(1024)S(1)}, s32[3072]{0:T(1024)}, u32[]{:S(2)}) copy-start(s32[3072]{0:T(1024)} %copy-done.91) | copy-start | bytes 36868
  518.2 36.7 %copy-start.96 = (f32[1,3072]{1,0:T(1,128)S(1)}, f32[1,3072]{1,0:T(1,128)}, u32[]{:S(2)}) copy-start(f32[1,3072]{1,0:T(1,128)} %get-tuple-element.156) | copy-start | bytes 36868
  533.7 21.2 %copy-start.97 = (f32[1,3072]{1,0:T(1,128)S(1)}, f32[1,3072]{1,0:T(1,128)}, u32[]{:S(2)}) copy-start(f32[1,3072]{1,0:T(1,128)} %get-tuple-element.158) | copy-start | bytes 36868
  533.7 34.7 %copy-start.85 = (f32[48,64]{1,0:T(8,128)S(1)}, f32[48,64]{1,0:T(8,128)}, u32[]{:S(2)}) copy-start(f32[48,64]{1,0:T(8,128)} %copy-done.80) | copy-start | bytes 36868
  546.1 25.7 %copy-start.54 = (f32[48,64]{1,0:T(8,128)S(1)}, f32[48,64]{1,0:T(8,128)}, u32[]{:S(2)}) copy-start(f32[48,64]{1,0:T(8,128)} %copy-done.53) | copy-start | bytes 36868
  546.1 25.7 %copy-start.9 = (f32[48,64]{1,0:T(8,128)S(1)}, f32[48,64]{1,0:T(8,128)}, u32[]{:S(2)}) copy-start(f32[48,64]{1,0:T(8,128)} %copy-done.7) | copy-start | bytes 36868
  546.1 25.7 %copy-start.12 = (f32[48,64]{1,0:T(8,128)S(1)}, f32[48,64]{1,0:T(8,128)}, u32[]{:S(2)}) copy-start(f32[48,64]{1,0:T(8,128)} %copy-done.10) | copy-start | bytes 36868
  546.1 25.7 %copy-start.15 = (f32[48,64]{1,0:T(8,128)S(1)}, f32[48,64]{1,0:T(8,128)}, u32[]{:S(2)}) copy-start(f32[48,64]{1,0:T(8,128)} %copy-done.13) | copy-start | bytes 36868
  546.1 25.7 %copy-start.60 = (f32[48,64]{1,0:T(8,128)S(1)}, f32[48,64]{1,0:T(8,128)}, u32[]{:S(2)}) copy-start(f32[48,64]{1,0:T(8,128)} %copy-done.58) | copy-start | bytes 36868
  546.1 25.7 %copy-start.63 = (f32[48,64]{1,0:T(8,128)S(1)}, f32[48,64]{1,0:T(8,128)}, u32[]{:S(2)}) copy-start(f32[48,64]{1,0:T(8,128)} %copy-done.61) | copy-start | bytes 36868
  556.8 15.3 %copy-start.170 = (f32[256]{0:T(256)S(1)}, f32[256]{0:T(256)}, u32[]{:S(2)}) copy-start(f32[256]{0:T(256)} %fusion.299) | copy-start | bytes 3076
  556.8 15.3 %copy-start.175 = (f32[256]{0:T(256)S(1)}, f32[256]{0:T(256)}, u32[]{:S(2)}) copy-start(f32[256]{0:T(256)} %fusion.301) | copy-start | bytes 3076
  572.1 13.5 %copy-start.33 = (f32[48,64,1]{1,0,2:T(8,128)S(1)}, f32[48,64,1]{1,0,2:T(8,128)}, u32[]{:S(2)}) copy-start(f32[48,64,1]{1,0,2:T(8,128)} %copy-done.31) | copy-start | bytes 36868
  592.7 5.2 collective-permute-start.4
  601.5 6.2 collective-permute-start.5
  632.8 34.3 %copy-start.1 = (f32[14,2048]{0,1:T(8,128)S(1)}, f32[14,2048]{0,1:T(8,128)}, u32[]{:S(2)}) copy-start(f32[14,2048]{0,1:T(8,128)} %multiply_add_fusion.7) | copy-start | bytes 344068
  633.3 75.8 %copy-start = (f32[2048,1,14]{2,1,0:T(1,128)S(1)}, f32[2048,1,14]{2,1,0:T(1,128)}, u32[]{:S(2)}) copy-start(f32[2048,1,14]{2,1,0:T(1,128)} %fusion.338) | copy-start | bytes 344068
  633.3 75.8 %copy-start.3 = (f32[14,2048]{0,1:T(8,128)S(1)}, f32[14,2048]{0,1:T(8,128)}, u32[]{:S(2)}) copy-start(f32[14,2048]{0,1:T(8,128)} %copy-done.2) | copy-start | bytes 344068
  (125 other events, 496.0 us)
